TPU v7x, 32 devices: a whole 2x2x4 slice. The times are simulated.
32 devices in a mesh: groups: 2 (over y), ctx: 4 (over z), tensor: 2 (over x), dp: 2 (over core).
Axes of the slice: x: 2, y: 2, z: 4, core: 2. Of those that a mesh axis runs over, the one named last changes fastest.
Arguments:
- tokens: bfloat16 [4, 1024, 1024], P(('groups', 'dp'), 'ctx', 'tensor'), parts along dimension 0
- w_qkv: bfloat16 [1024, 3, 1024], P(None, None, 'tensor')
- w_out: bfloat16 [1024, 1024], P('tensor'), may hold values from -0.1875 to 0.1875
- labels: int32 [4, 8, 1024], P(('groups', 'dp'), 'tensor', 'ctx'), parts along dimension 0, may hold values from 0 to 255, as said below
- grad_out: bfloat16 [4, 1024, 1024], P(('groups', 'dp'), 'ctx', 'tensor'), parts along dimension 0, may hold values from -6 to 6
Outputs:
- attended: bfloat16 [4, 1024, 1024], P(('groups', 'dp'), 'ctx', 'tensor'), parts along dimension 0
- grad_tokens: bfloat16 [4, 1024, 1024], P(('groups', 'dp'), 'ctx', 'tensor'), parts along dimension 0
- grad_w_qkv: float32 [2048, 3, 1024], P('groups', None, 'tensor'), parts along dimension 0
- grad_w_out: float32 [2048, 1024], P(('groups', 'tensor')), parts along dimension 0
There are 2 independent parts, one for each index of `groups`. A program takes and returns all parts, laid end to end along the dimension named above; an argument that names none is the same for every part. Nothing has to cross between parts.
Inputs may be any that keep to these rules, and one draw needn't show every extreme that they name: `labels`: cluster c of any head belongs to owner c % 4. Among the 256 tokens of one document on one index of ctx, at most 192 have, for one head, clusters of one owner; for each head one owner has exactly 192 from every such block, and the other owners share the rest of a block evenly (counts differ by at most one).
All inputs are finite; a program needn't handle non-finite values.
Results may differ from a plain program's by a relative error of at most 0.035.
The roundings to bfloat16 on the way count: a program that leaves them out, or rounds other values in their place, can miss the bound.
Values may be sent and summed in bfloat16 or wider, within the bound.
A program may use at most 64 MiB of HBM per device.

v0:
```python
import math
import jax
import jax.numpy as jnp
from jax import lax
from jax.sharding import PartitionSpec as P

HD = 128


def contract_last(left, right):
    return lax.dot_general(
        left, right, (((1,), (1,)), ((), ())), preferred_element_type=jnp.float32
    )


def contract_first(left, right):
    return lax.dot_general(
        left, right, (((0,), (0,)), ((), ())), preferred_element_type=jnp.float32
    )


def masked_probs(query_block, label_block, keys_in, marks):
    scores = contract_last(query_block, keys_in) * HD ** (-0.5)
    same = label_block[:, None] == marks[None, :]
    scores = jnp.where(same, scores, jnp.float32(-1e30))
    top_value = jnp.max(scores, axis=1, keepdims=True)
    expo = jnp.exp(scores - top_value)
    return expo / jnp.sum(expo, axis=1, keepdims=True)


def owner_forward(queries, keys_in, values_in, marks):
    total = queries.shape[0]
    block_rows = math.gcd(total, 512)
    block_count = total // block_rows

    def forward_block(index):
        start = index * block_rows
        query_block = lax.dynamic_slice_in_dim(queries, start, block_rows, 0)
        label_block = lax.dynamic_slice_in_dim(marks, start, block_rows, 0)
        probs = masked_probs(query_block, label_block, keys_in, marks).astype(jnp.bfloat16)
        return jnp.dot(probs, values_in, preferred_element_type=jnp.float32).astype(jnp.bfloat16)

    return lax.map(forward_block, jnp.arange(block_count, dtype=jnp.int32)).reshape(
        total, queries.shape[1]
    )


def owner_backward(queries, keys_in, values_in, marks, attention, cotangent):
    total, size = queries.shape
    block_rows = math.gcd(total, 512)
    block_count = total // block_rows

    def backward_block(carry, index):
        grad_keys, grad_values = carry
        start = index * block_rows
        query_block = lax.dynamic_slice_in_dim(queries, start, block_rows, 0)
        label_block = lax.dynamic_slice_in_dim(marks, start, block_rows, 0)
        attn_block = lax.dynamic_slice_in_dim(attention, start, block_rows, 0)
        cot_block = lax.dynamic_slice_in_dim(cotangent, start, block_rows, 0)
        probs_full = masked_probs(query_block, label_block, keys_in, marks)
        probs = probs_full.astype(jnp.bfloat16)
        dprob = contract_last(cot_block, values_in)
        delta = jnp.sum(
            cot_block.astype(jnp.float32) * attn_block.astype(jnp.float32), axis=1, keepdims=True
        )
        dscore = (probs_full * (dprob - delta) * HD ** (-0.5)).astype(jnp.bfloat16)
        grad_query = jnp.dot(dscore, keys_in, preferred_element_type=jnp.float32).astype(
            jnp.bfloat16
        )
        grad_keys = grad_keys + contract_first(dscore, query_block)
        grad_values = grad_values + contract_first(probs, cot_block)
        return ((grad_keys, grad_values), grad_query)

    empty = jnp.zeros((total, size), jnp.float32)
    (grad_keys, grad_values), grad_queries = lax.scan(
        backward_block, (empty, empty), jnp.arange(block_count, dtype=jnp.int32)
    )
    return (
        grad_queries.reshape(total, size),
        grad_keys.astype(jnp.bfloat16),
        grad_values.astype(jnp.bfloat16),
    )


def shards(tokens, w_qkv, w_out, labels, grad_out):
    rows_all, grads_all = (
        lax.all_gather(tokens, "tensor", axis=2, tiled=True),
        lax.all_gather(grad_out, "tensor", axis=2, tiled=True),
    )
    tok_rows = rows_all[0]
    tok_grads = grads_all[0]
    tok_count, width = tok_rows.shape
    heads_local = w_out.shape[0] // HD
    ctx_count = lax.axis_size("ctx")
    capacity = 3 * tok_count // ctx_count
    slot_total = ctx_count * capacity
    qkv = jnp.dot(
        tok_rows, w_qkv.reshape(width, 3 * heads_local * HD), preferred_element_type=jnp.float32
    )
    qkv = qkv.astype(jnp.bfloat16).reshape(tok_count, 3, heads_local, HD)
    qkv_heads = jnp.transpose(qkv, (2, 0, 1, 3)).reshape(heads_local, tok_count, 3 * HD)
    cotangent = contract_last(tok_grads, w_out).astype(jnp.bfloat16)
    cot_heads = jnp.transpose(cotangent.reshape(tok_count, heads_local, HD), (1, 0, 2))
    labels_local = labels[0]
    owner_of = labels_local % ctx_count
    owner_hits = (
        owner_of[:, :, None] == jnp.arange(ctx_count, dtype=jnp.int32)[None, None, :]
    ).astype(jnp.int32)
    earlier = jnp.cumsum(owner_hits, axis=1) - owner_hits
    slot_index = jnp.sum(earlier * owner_hits, axis=2)
    destination = owner_of * capacity + slot_index

    def pack(values):
        feature_count = values.shape[2]
        empty_buffer = jnp.zeros((heads_local, slot_total, feature_count), values.dtype)
        filled = jax.vmap(lambda buffer, where_to, rows_in: buffer.at[where_to].set(rows_in))(
            empty_buffer, destination, values
        )
        return filled.reshape(heads_local, ctx_count, capacity, feature_count)

    def unpack(received):
        flat = received.reshape(heads_local, slot_total, received.shape[3])
        return jax.vmap(lambda table, where_to: jnp.take(table, where_to, axis=0))(
            flat, destination
        )

    label_slots = jax.vmap(
        lambda where_to, marks: jnp.full((slot_total,), -1.0, jnp.bfloat16).at[where_to].set(marks)
    )(destination, labels_local.astype(jnp.bfloat16)).reshape(heads_local, ctx_count, capacity)
    arrived, arrived_marks = (
        lax.all_to_all(pack(qkv_heads), "ctx", split_axis=1, concat_axis=1, tiled=True),
        lax.all_to_all(label_slots, "ctx", split_axis=1, concat_axis=1, tiled=True),
    )
    arrived = arrived.reshape(heads_local, slot_total, 3 * HD)
    marks_own = arrived_marks.reshape(heads_local, slot_total)
    queries_own = arrived[:, :, :HD]
    keys_own = arrived[:, :, HD : 2 * HD]
    values_own = arrived[:, :, 2 * HD :]
    attention_own = jax.vmap(owner_forward)(queries_own, keys_own, values_own, marks_own)
    returned = lax.all_to_all(
        attention_own.reshape(heads_local, ctx_count, capacity, HD),
        "ctx",
        split_axis=1,
        concat_axis=1,
        tiled=True,
    )
    attention_tok = unpack(returned)
    cot_arrived = lax.all_to_all(pack(cot_heads), "ctx", split_axis=1, concat_axis=1, tiled=True)
    cot_own = cot_arrived.reshape(heads_local, slot_total, HD)
    grad_q, grad_k, grad_v = jax.vmap(owner_backward)(
        queries_own, keys_own, values_own, marks_own, attention_own, cot_own
    )
    grads_own = jnp.concatenate([grad_q, grad_k, grad_v], axis=2).reshape(
        heads_local, ctx_count, capacity, 3 * HD
    )
    grads_back = lax.all_to_all(grads_own, "ctx", split_axis=1, concat_axis=1, tiled=True)
    grad_heads = unpack(grads_back)
    attention_rows = jnp.transpose(attention_tok, (1, 0, 2)).reshape(tok_count, heads_local * HD)
    out_terms = jnp.dot(attention_rows, w_out, preferred_element_type=jnp.float32)
    attended = lax.psum_scatter(
        out_terms.astype(jnp.bfloat16), "tensor", scatter_dimension=1, tiled=True
    )
    grad_qkv = jnp.transpose(grad_heads.reshape(heads_local, tok_count, 3, HD), (1, 2, 0, 3))
    grad_qkv = grad_qkv.reshape(tok_count, 3 * heads_local * HD)
    grad_w_out_local = contract_first(attention_rows, tok_grads)
    grad_w_qkv_local = contract_first(tok_rows, grad_qkv).reshape(width, 3, heads_local * HD)
    summed_qkv, summed_out = (
        lax.psum(grad_w_qkv_local.astype(jnp.bfloat16), ("ctx", "dp")).astype(jnp.float32),
        lax.psum(grad_w_out_local.astype(jnp.bfloat16), ("ctx", "dp")).astype(jnp.float32),
    )
    in_terms = contract_last(grad_qkv, w_qkv.reshape(width, 3 * heads_local * HD))
    grad_tokens = lax.psum_scatter(
        in_terms.astype(jnp.bfloat16), "tensor", scatter_dimension=1, tiled=True
    )
    return (attended[None], grad_tokens[None], summed_qkv, summed_out)


def solution(mesh):
    placed = (
        P(("groups", "dp"), "ctx", "tensor"),
        P(None, None, "tensor"),
        P("tensor", None),
        P(("groups", "dp"), "tensor", "ctx"),
        P(("groups", "dp"), "ctx", "tensor"),
    )
    return jax.shard_map(
        shards,
        mesh=mesh,
        in_specs=placed,
        out_specs=(
            P(("groups", "dp"), "ctx", "tensor"),
            P(("groups", "dp"), "ctx", "tensor"),
            P("groups", None, "tensor"),
            P(("groups", "tensor"), None),
        ),
        check_vma=False,
    )
```

profile of v0, /device:TPU:0, one launch (start us, length us, event | category | flops | bytes accessed | tf_op | source)
XLA Modules:
  0.0 419.2 jit_solution(18375576288930993019)
XLA Ops:
  10.2 4.8 %reduce-window.6 = s32[4,4,2,128]{3,2,1,0:T(2,128)S(1)} reduce-window(s32[4,4,2,128]{3,2,1,0:T(2,128)S(1)} %compare_convert_fusion, s32[]{:T(128)} %constant.96.clone.1), window={size=1x1x1x128 pad=0_0x0_0x0_0x127_0}, to_apply=%region_0.1 | reduce-window | flops 520192 | bytes 32772 | tf_op jit(solution)/shard_map/reduce-window
  17.8 7.6 %scatter_custom_fusion = bf16[3072]{0:T(1024)(128)(2,1)S(1)} fusion(s32[1024]{0:T(1024)S(1)} %bitcast.228, bf16[1024]{0:T(1024)(128)(2,1)S(1)} %bitcast.231, bf16[]{:T(256)} %constant.103.clone.1), kind=kCustom, calls=%fused_computation.120 | custom fusion | bytes 6146
  26.1 6.3 %all-to-all-start = ((bf16[4,4,192]{2,0,1:T(4,128)(2,1)}), bf16[4,4,192]{2,0,1:T(4,128)(2,1)S(1)}, u32[]{:S(2)}, u32[]{:S(2)}) async-start(bf16[4,4,192]{2,0,1:T(4,128)(2,1)} %copy.67), calls=%async_computation | async-start | bytes 16384 | tf_op jit(solution)/shard_map/all_to_all | solution.py:132
  32.4 8.6 %all_gather.7 = bf16[1,256,1024]{2,1,0:T(8,128)(2,1)S(1)} all-gather(bf16[1,256,512]{2,1,0:T(8,128)(2,1)} %param.13), channel_id=1, replica_groups=mesh['groups'=2,'ctx'=4,'tensor'=2,'dp'=2] {'tensor'}, dimensions={2}, use_global_device_ids=true | all-gather | bytes 786432 | tf_op jit(solution)/shard_map/all_gather | solution.py:88
  42.4 3.4 scatter_custom_fusion.2
  46.8 4.8 %all-to-all-start.3 = ((bf16[4,4,192,128]{3,2,0,1:T(8,128)(2,1)}), bf16[4,4,192,128]{3,2,0,1:T(8,128)(2,1)}, u32[]{:S(2)}, u32[]{:S(2)}) async-start(bf16[4,4,192,128]{3,2,0,1:T(8,128)(2,1)} %copy.80), calls=%async_computation.4 | async-start | bytes 1572864 | tf_op jit(solution)/shard_map/all_to_all | solution.py:148
  51.6 4.7 %copy.69 = bf16[1024,3,512]{0,2,1:T(8,128)(2,1)} copy(bf16[1024,3,512]{2,0,1:T(8,128)(2,1)} %param.10) | data formatting | bytes 6291456 | tf_op args[1]
  56.3 7.0 %all_gather.6 = bf16[1,256,1024]{2,1,0:T(8,128)(2,1)S(1)} all-gather(bf16[1,256,512]{2,1,0:T(8,128)(2,1)S(1)} %copy-done.10), channel_id=1, replica_groups=mesh['groups'=2,'ctx'=4,'tensor'=2,'dp'=2] {'tensor'}, dimensions={2}, use_global_device_ids=true | all-gather | bytes 786432 | tf_op jit(solution)/shard_map/all_gather | solution.py:87
  64.1 2.9 convolution_convert_fusion.2
  69.3 6.5 %scatter_custom_fusion.1 = bf16[3072,384]{1,0:T(8,128)(2,1)S(1)} fusion(s32[1024]{0:T(1024)S(1)} %bitcast.230, bf16[1024,384]{1,0:T(8,128)(2,1)} %copy.71, bf16[]{:T(256)} %constant.102.clone.1), kind=kCustom, calls=%fused_computation.77 | custom fusion | bytes 2359808
  75.8 1.7 copy.72
  77.5 5.1 %all-to-all-start.1 = ((bf16[4,4,192,384]{3,2,0,1:T(8,128)(2,1)}), bf16[4,4,192,384]{3,2,0,1:T(8,128)(2,1)}, u32[]{:S(2)}, u32[]{:S(2)}) async-start(bf16[4,4,192,384]{3,2,0,1:T(8,128)(2,1)} %copy.72), calls=%async_computation.1 | async-start | bytes 4718592 | tf_op jit(solution)/shard_map/all_to_all | solution.py:131
  82.9 2.1 copy.81
  85.0 48.7 %all-to-all-done.1 = bf16[4,4,192,384]{3,2,0,1:T(8,128)(2,1)} async-done(((bf16[4,4,192,384]{3,2,0,1:T(8,128)(2,1)}), bf16[4,4,192,384]{3,2,0,1:T(8,128)(2,1)}, u32[]{:S(2)}, u32[]{:S(2)}) %all-to-all-start.1) | async-done | bytes 2359328 | tf_op jit(solution)/shard_map/all_to_all | solution.py:131
  133.7 1.9 copy.73
  137.4 23.0 %while.33 = (s32[]{:T(128)}, bf16[3,4,256,128]{3,2,0,1:T(8,128)(2,1)S(1)}, s32[3]{0:T(128)S(1)}, bf16[4,768]{1,0:T(4,128)(2,1)S(1)}, bf16[4,4,192]{2,1,0:T(4,128...) while((s32[]{:T(128)}, ...), condition=%wide.wide.region_8.9_spmd, body=%wide.wide.region_5.8_spmd.sunk | while | flops 612764160 | bytes 3175139 | solution.py:43
  138.8 2.5 fusion.172
  141.3 3.8 fusion.173
  146.5 2.5 fusion.172
  149.0 3.8 fusion.173
  154.1 2.5 fusion.172
  156.6 3.8 fusion.173
  161.4 4.2 all-to-all-start.2
  166.7 56.3 %while.34 = (s32[]{:T(128)}, f32[4,768,128]{2,1,0:T(8,128)S(1)}, f32[4,768,128]{2,1,0:T(8,128)}, bf16[3,4,256,128]{3,2,0,1:T(8,128)(2,1)}, s32[3]{0:T(128)S(1)},...) while((s32[]{:T(128)}, f32[4,768,128]{2,1,0:T(8,128)S(1)}, ...), condition=%wide.wide.region_15.16_spmd.clone, body=%wide.wide.region_11.15_spmd.clone.sunk | while | flops 1222772224 | bytes 25732404 | solution.py:75
  169.2 4.1 fusion.187
  173.3 3.0 multiply_convert_fusion.3
  177.6 2.2 select_add_fusion.6
  179.9 5.2 %select_add_fusion.7 = f32[4,768,128]{2,1,0:T(8,128)} fusion(f32[4,768,128]{2,1,0:T(8,128)} %get-tuple-element.590, f32[4,256]{1,0:T(4,128)S(1)} %get-tuple-element.527, pred[]{:T(512)S(6)} %compare.29, bf16[4,768,128]{2,1,0:T(8,128)(2,1)} %get-tuple-element.615, s32[]{:T(128)S(1)} %bitcast.226, ...), kind=kOutput, calls=%fused_computation.37.clone.clone.1 | convolution fusion | flops 408160000 | bytes 4469761 | tf_op jit(solution)/shard_map/vmap()/while/body/eval_jaxpr/dot_general | solution.py:17
  187.6 4.1 fusion.187
  191.7 3.0 multiply_convert_fusion.3
  196.0 2.2 select_add_fusion.6
  198.3 5.7 %select_add_fusion.7 = f32[4,768,128]{2,1,0:T(8,128)} fusion(f32[4,768,128]{2,1,0:T(8,128)} %get-tuple-element.590, f32[4,256]{1,0:T(4,128)S(1)} %get-tuple-element.527, pred[]{:T(512)S(6)} %compare.29, bf16[4,768,128]{2,1,0:T(8,128)(2,1)} %get-tuple-element.615, s32[]{:T(128)S(1)} %bitcast.226, ...), kind=kOutput, calls=%fused_computation.37.clone.clone.1 | convolution fusion | flops 408160000 | bytes 4469761 | tf_op jit(solution)/shard_map/vmap()/while/body/eval_jaxpr/dot_general | solution.py:17
  206.6 4.1 fusion.187
  210.7 3.0 multiply_convert_fusion.3
  215.0 2.2 select_add_fusion.6
  217.2 5.7 %select_add_fusion.7 = f32[4,768,128]{2,1,0:T(8,128)} fusion(f32[4,768,128]{2,1,0:T(8,128)} %get-tuple-element.590, f32[4,256]{1,0:T(4,128)S(1)} %get-tuple-element.527, pred[]{:T(512)S(6)} %compare.29, bf16[4,768,128]{2,1,0:T(8,128)(2,1)} %get-tuple-element.615, s32[]{:T(128)S(1)} %bitcast.226, ...), kind=kOutput, calls=%fused_computation.37.clone.clone.1 | convolution fusion | flops 408160000 | bytes 4469761 | tf_op jit(solution)/shard_map/vmap()/while/body/eval_jaxpr/dot_general | solution.py:17
  226.0 1.7 copy.84
  227.6 5.2 %all-to-all-start.4 = ((bf16[4,4,192,384]{3,2,0,1:T(8,128)(2,1)}), bf16[4,4,192,384]{3,2,0,1:T(8,128)(2,1)}, u32[]{:S(2)}, u32[]{:S(2)}) async-start(bf16[4,4,192,384]{3,2,0,1:T(8,128)(2,1)} %copy.84), calls=%async_computation.5 | async-start | bytes 4718592 | tf_op jit(solution)/shard_map/all_to_all | solution.py:156
  234.1 5.8 %gather_fusion = bf16[1024,128]{1,0:T(8,128)(2,1)S(1)} fusion(bf16[4,768,128]{2,1,0:T(8,128)(2,1)S(1)} %bitcast.205, s32[1024]{0:T(1024)S(1)} %bitcast.199), kind=kCustom, calls=%fused_computation | custom fusion | bytes 532480 | tf_op jit(solution)/shard_map/vmap(jit(_take))/gather | solution.py:123
  242.3 43.4 %all-to-all-done.4 = bf16[4,4,192,384]{3,2,0,1:T(8,128)(2,1)} async-done(((bf16[4,4,192,384]{3,2,0,1:T(8,128)(2,1)}), bf16[4,4,192,384]{3,2,0,1:T(8,128)(2,1)}, u32[]{:S(2)}, u32[]{:S(2)}) %all-to-all-start.4) | async-done | bytes 2359328 | tf_op jit(solution)/shard_map/all_to_all | solution.py:156
  285.7 1.9 copy.85
  287.6 11.6 %gather_fusion.1 = bf16[1024,384]{1,0:T(8,128)(2,1)} fusion(bf16[4,768,384]{2,1,0:T(8,128)(2,1)S(1)} %bitcast.201, s32[1024]{0:T(1024)S(1)} %bitcast.200), kind=kCustom, calls=%fused_computation.1 | custom fusion | bytes 1581056 | tf_op jit(solution)/shard_map/vmap(jit(_take))/gather | solution.py:123
  301.7 2.7 convolution_convert_fusion.1
  304.4 4.7 %copy.88 = bf16[1024,3,512]{2,0,1:T(8,128)(2,1)} copy(bf16[1024,3,512]{0,2,1:T(8,128)(2,1)} %bitcast.202) | data formatting | bytes 6291456 | tf_op jit(solution)/shard_map/convert_element_type | solution.py:168
  311.3 3.7 convolution_convert_fusion.5
  315.1 90.2 %all-reduce.3.cloned.1.call-done = (bf16[1024,3,512]{2,0,1:T(8,128)(2,1)}, bf16[512,1024]{1,0:T(8,128)(2,1)}) async-done(((bf16[1024,3,512]{2,0,1:T(8,128)(2,1)}, bf16[512,1024]{1,0:T(8,128)(2,1)}), (bf16[1024,3,512]{2,0,1:T(8,128)(2,1)}, bf16[512,1024]{1,0:T(8,128)(2,1)})) %all-reduce.3.cloned.1.call-update) | async-done | bytes 4194320 | tf_op jit(solution)/shard_map/psum | solution.py:168
  405.3 2.9 convert_element_type.81
  408.2 3.6 convert_element_type.79
  (120 shorter events, 37.9 us)
Async XLA Ops:
  8.0 33.8 %copy-start = (bf16[512,1024]{1,0:T(8,128)(2,1)S(1)}, bf16[512,1024]{1,0:T(8,128)(2,1)}, u32[]{:S(2)}) copy-start(bf16[512,1024]{1,0:T(8,128)(2,1)} %param.11) | copy-start | bytes 3145732
  26.1 20.7 %all-to-all-start = ((bf16[4,4,192]{2,0,1:T(4,128)(2,1)}), bf16[4,4,192]{2,0,1:T(4,128)(2,1)S(1)}, u32[]{:S(2)}, u32[]{:S(2)}) async-start(bf16[4,4,192]{2,0,1:T(4,128)(2,1)} %copy.67), calls=%async_computation | async-start | bytes 16384 | tf_op jit(solution)/shard_map/all_to_all | solution.py:132
  41.0 0.8 copy-start.1
  46.8 30.7 %all-to-all-start.3 = ((bf16[4,4,192,128]{3,2,0,1:T(8,128)(2,1)}), bf16[4,4,192,128]{3,2,0,1:T(8,128)(2,1)}, u32[]{:S(2)}, u32[]{:S(2)}) async-start(bf16[4,4,192,128]{3,2,0,1:T(8,128)(2,1)} %copy.80), calls=%async_computation.4 | async-start | bytes 1572864 | tf_op jit(solution)/shard_map/all_to_all | solution.py:148
  51.6 4.7 %copy-start.10 = (bf16[1,256,512]{2,1,0:T(8,128)(2,1)S(1)}, bf16[1,256,512]{2,1,0:T(8,128)(2,1)}, u32[]{:S(2)}) copy-start(bf16[1,256,512]{2,1,0:T(8,128)(2,1)} %param.9) | copy-start | bytes 786436
  63.3 0.8 copy-start.6
  77.5 56.2 %all-to-all-start.1 = ((bf16[4,4,192,384]{3,2,0,1:T(8,128)(2,1)}), bf16[4,4,192,384]{3,2,0,1:T(8,128)(2,1)}, u32[]{:S(2)}, u32[]{:S(2)}) async-start(bf16[4,4,192,384]{3,2,0,1:T(8,128)(2,1)} %copy.72), calls=%async_computation.1 | async-start | bytes 4718592 | tf_op jit(solution)/shard_map/all_to_all | solution.py:131
  82.6 53.0 %copy-start.11 = (bf16[4,4,192]{2,1,0:T(4,128)(2,1)}, bf16[4,4,192]{2,1,0:T(4,128)(2,1)S(1)}, u32[]{:S(2)}) copy-start(bf16[4,4,192]{2,1,0:T(4,128)(2,1)S(1)} %copy.68) | copy-start | bytes 18436
  161.4 66.2 %all-to-all-start.2 = ((bf16[4,4,192,128]{3,2,0,1:T(8,128)(2,1)}), bf16[4,4,192,128]{3,2,0,1:T(8,128)(2,1)}, u32[]{:S(2)}, u32[]{:S(2)}) async-start(bf16[4,4,192,128]{3,2,0,1:T(8,128)(2,1)} %copy.76), calls=%async_computation.2 | async-start | bytes 1572864 | tf_op jit(solution)/shard_map/all_to_all | solution.py:140
  173.3 3.0 copy-start.9
  191.7 3.0 copy-start.9
  210.7 3.0 copy-start.9
  223.0 1.4 copy-start.8
  227.6 5.2 %copy-start.12 = (s32[1,4,256]{2,1,0:T(4,128)S(1)}, s32[1,4,256]{2,1,0:T(4,128)}, u32[]{:S(2)}) copy-start(s32[1,4,256]{2,1,0:T(4,128)} %param.12) | copy-start | bytes 12292
  227.6 58.0 %all-to-all-start.4 = ((bf16[4,4,192,384]{3,2,0,1:T(8,128)(2,1)}), bf16[4,4,192,384]{3,2,0,1:T(8,128)(2,1)}, u32[]{:S(2)}, u32[]{:S(2)}) async-start(bf16[4,4,192,384]{3,2,0,1:T(8,128)(2,1)} %copy.84), calls=%async_computation.5 | async-start | bytes 4718592 | tf_op jit(solution)/shard_map/all_to_all | solution.py:156
  232.8 8.0 %copy-start.2 = (bf16[1,256,1024]{2,1,0:T(8,128)(2,1)S(1)}, bf16[1,256,1024]{2,1,0:T(8,128)(2,1)}, u32[]{:S(2)}) copy-start(bf16[1,256,1024]{2,1,0:T(8,128)(2,1)} %copy-done.1) | copy-start | bytes 1572868
  232.8 172.4 %all-reduce.3.cloned.1.call-start = ((), (), s32[]{:S(2)}) async-start(), calls=%async_computation.9 | async-start | bytes 8388608 | tf_op jit(solution)/shard_map/psum | solution.py:168
  240.2 0.7 copy-start.4
  299.2 2.5 copy-start.7
  309.1 0.9 copy-start.5
  309.1 102.7 %reduce-scatter.3.cloned.1.call-start = ((), (), s32[]{:S(2)}) async-start(), calls=%async_computation.7 | async-start | bytes 786432 | tf_op jit(solution)/shard_map/reduce_scatter | solution.py:160
  311.3 100.5 %reduce-scatter.5.cloned.1.call-start = ((), (), s32[]{:S(2)}) async-start(), calls=%async_computation.8 | async-start | bytes 786432 | tf_op jit(solution)/shard_map/reduce_scatter | solution.py:172
  405.2 2.9 copy-start.3
Sparse Core Ops, SparseCore 0:
  309.2 95.9 all-reduce.2
Sparse Core Ops, SparseCore 1:
  312.4 13.6 reduce-scatter.2
  328.8 14.5 reduce-scatter.4
where the time goes:
time: 421 us; the launch traced here: 419 us
  waiting for transfers between devices  182 us (43%)
  matrix products  80 us (19%)
  local copies, waits for them, and re-layouts  74.3 us (18%)
  starting transfers between devices  25.7 us (6%)
  other arithmetic  21.4 us (5%)
  between operations  15.8 us (4%)
  blocking collectives  15.7 us (4%)
    psum x1, waiting for transfers between devices, shards(): lax.psum(grad_w_qkv_local.astype(jnp.bfloat16), ('ctx', 'dp'))  90.2 us
    all_to_all x1, waiting for transfers between devices, shards(): lax.all_to_all(pack(qkv_heads), 'ctx', split_axis=1, concat_axis=1, tiled...  48.7 us
    all_to_all x1, waiting for transfers between devices, shards(): lax.all_to_all(grads_own, 'ctx', split_axis=1, concat_axis=1, tiled=True)  43.4 us
    dot_general x8, matrix products, contract_first(): lax.dot_general(left, right, (((0,), (0,)), ((), ())), preferred_element_...  27.5 us
    unnamed x32, local copies, waits for them, and re-layouts  26.9 us
    sub x6, matrix products, masked_probs(): expo = jnp.exp(scores - top_value)  19.8 us
    gather x5, local copies, waits for them, and re-layouts, unpack(): jnp.take(table, where_to, axis=0)  19.6 us
    dot_general x5, matrix products, contract_last(): lax.dot_general(left, right, (((1,), (1,)), ((), ())), preferred_element_...  13.2 us
  transfers between devices with their start and end apart: 8, of which 3 were waited for; matrix products, arithmetic and copies ran while one was open for 25% of the time, Pallas kernels for 0%

commit v1 on v0

--- a/solution.py
+++ b/solution.py
@@ -5,6 +5,29 @@
 from jax.sharding import PartitionSpec as P
 
 HD = 128
+
+
+def cut_along(value, dim, size):
+    dims = value.shape
+    tiles = value.reshape(*dims[:dim], size, dims[dim] // size, *dims[dim + 1 :])
+    return jnp.moveaxis(tiles, dim, 0)
+
+
+def in_order(blocks, dim):
+    shape = list(blocks.shape[1:])
+    shape[dim] *= blocks.shape[0]
+    return jnp.moveaxis(blocks, 0, dim).reshape(shape)
+
+
+def exchange_in_pairs(array, axis, split_dim, concat_dim):
+    size, index = (lax.axis_size(axis), lax.axis_index(axis))
+    tiles = cut_along(array, split_dim, size)
+    outs = [tiles[index]]
+    for step in range(1, size):
+        sent = tiles[index ^ step]
+        outs.append(lax.ppermute(sent, axis, [(i, i ^ step) for i in range(size)]))
+    tiles = jnp.stack(outs)[index ^ jnp.arange(size)]
+    return in_order(tiles, concat_dim)
 
 
 def contract_last(left, right):
@@ -128,7 +151,7 @@
         lambda where_to, marks: jnp.full((slot_total,), -1.0, jnp.bfloat16).at[where_to].set(marks)
     )(destination, labels_local.astype(jnp.bfloat16)).reshape(heads_local, ctx_count, capacity)
     arrived, arrived_marks = (
-        lax.all_to_all(pack(qkv_heads), "ctx", split_axis=1, concat_axis=1, tiled=True),
+        exchange_in_pairs(pack(qkv_heads), "ctx", 1, 1),
         lax.all_to_all(label_slots, "ctx", split_axis=1, concat_axis=1, tiled=True),
     )
     arrived = arrived.reshape(heads_local, slot_total, 3 * HD)

time: 421 us -> 400 us (0.950)
  waiting for transfers between devices: 182 us -> 156 us
    all_to_all x1 -> x0, waiting for transfers between devices: 48.7 us -> none  [shards(): lax.all_to_all(pack(qkv_heads), 'ctx', split_axis=1, concat_axis=1, tiled...]
    all_to_all x1, waiting for transfers between devices: 0.01 us -> 21.7 us  [shards(): lax.all_to_all(label_slots, 'ctx', split_axis=1, concat_axis=1, tiled=True)]
    all_to_all x1 -> x0, starting transfers between devices: 5.09 us -> none  [shards(): lax.all_to_all(pack(qkv_heads), 'ctx', split_axis=1, concat_axis=1, tiled...]
    ppermute x0 -> x3, starting transfers between devices: none -> 4.39 us  [exchange_in_pairs(): outs.append(lax.ppermute(sent, axis, [(i, i ^ step) for i in range(size)]))]
    unnamed x32 -> x30, local copies, waits for them, and re-layouts: 26.9 us -> 25.7 us
  transfers between devices with their start and end apart: 8 -> 10, of which waited for: 3 -> 3; matrix products, arithmetic and copies ran while one was open for 25% -> 32% of each run, Pallas kernels for 0% -> 0%
where the time goes in v1:
time: 400 us; the launch traced here: 398 us
  waiting for transfers between devices  156 us (39%)
  matrix products  79.9 us (20%)
  local copies, waits for them, and re-layouts  77.3 us (19%)
  other arithmetic  24.1 us (6%)
  starting transfers between devices  23.9 us (6%)
  blocking collectives  17.6 us (4%)
  between operations  15.8 us (4%)
  loops' own time  4.09 us (1%)
    psum x1, waiting for transfers between devices, shards(): lax.psum(grad_w_qkv_local.astype(jnp.bfloat16), ('ctx', 'dp'))  90.2 us
    all_to_all x1, waiting for transfers between devices, shards(): lax.all_to_all(grads_own, 'ctx', split_axis=1, concat_axis=1, tiled=True)  43.6 us
    dot_general x8, matrix products, contract_first(): lax.dot_general(left, right, (((0,), (0,)), ((), ())), preferred_element_...  27.4 us
    unnamed x30, local copies, waits for them, and re-layouts  25.7 us
    all_to_all x1, waiting for transfers between devices, shards(): lax.all_to_all(label_slots, 'ctx', split_axis=1, concat_axis=1, tiled=True)  21.7 us
    sub x6, matrix products, masked_probs(): expo = jnp.exp(scores - top_value)  19.8 us
    gather x5, local copies, waits for them, and re-layouts, unpack(): jnp.take(table, where_to, axis=0)  19.5 us
    dot_general x5, matrix products, contract_last(): lax.dot_general(left, right, (((1,), (1,)), ((), ())), preferred_element_...  13.2 us
  transfers between devices with their start and end apart: 10, of which 3 were waited for; matrix products, arithmetic and copies ran while one was open for 32% of the time, Pallas kernels for 0%

profile of v1, /device:TPU:0, one launch (start us, length us, event | category | flops | bytes accessed | tf_op | source)
XLA Modules:
  0.0 398.3 jit_solution(16426957476552359317)
XLA Ops:
  9.5 4.8 %reduce-window.6 = s32[4,4,2,128]{3,2,1,0:T(2,128)S(1)} reduce-window(s32[4,4,2,128]{3,2,1,0:T(2,128)S(1)} %compare_convert_fusion, s32[]{:T(128)} %constant.82.clone.1), window={size=1x1x1x128 pad=0_0x0_0x0_0x127_0}, to_apply=%region_0.1 | reduce-window | flops 520192 | bytes 32772 | tf_op jit(solution)/shard_map/reduce-window
  17.1 10.2 %all_gather.6 = bf16[1,256,1024]{2,1,0:T(8,128)(2,1)S(1)} all-gather(bf16[1,256,512]{2,1,0:T(8,128)(2,1)} %param.9), channel_id=1, replica_groups=mesh['groups'=2,'ctx'=4,'tensor'=2,'dp'=2] {'tensor'}, dimensions={2}, use_global_device_ids=true | all-gather | bytes 786432 | tf_op jit(solution)/shard_map/all_gather | solution.py:110
  27.3 4.8 %copy.70 = bf16[1024,3,512]{0,2,1:T(8,128)(2,1)} copy(bf16[1024,3,512]{2,0,1:T(8,128)(2,1)} %param.10) | data formatting | bytes 6291456 | tf_op args[1]
  32.1 2.9 convolution_convert_fusion.2
  37.3 6.3 %scatter_custom_fusion.1 = bf16[3072,384]{1,0:T(8,128)(2,1)S(1)} fusion(s32[1024]{0:T(1024)S(1)} %bitcast.247, bf16[1024,384]{1,0:T(8,128)(2,1)} %copy.72, bf16[]{:T(256)} %constant.110.clone.1), kind=kCustom, calls=%fused_computation.79 | custom fusion | bytes 2359808
  45.1 3.8 collective-permute-start.2
  49.5 7.6 %scatter_custom_fusion = bf16[3072]{0:T(1024)(128)(2,1)S(1)} fusion(s32[1024]{0:T(1024)S(1)} %bitcast.248, bf16[1024]{0:T(1024)(128)(2,1)S(1)} %bitcast.250, bf16[]{:T(256)} %constant.115.clone.1), kind=kCustom, calls=%fused_computation.127 | custom fusion | bytes 6146
  57.8 5.1 %all-to-all-start = ((bf16[4,4,192]{2,0,1:T(4,128)(2,1)}), bf16[4,4,192]{2,0,1:T(4,128)(2,1)S(1)}, u32[]{:S(2)}, u32[]{:S(2)}) async-start(bf16[4,4,192]{2,0,1:T(4,128)(2,1)} %copy.68), calls=%async_computation | async-start | bytes 16384 | tf_op jit(solution)/shard_map/all_to_all | solution.py:155
  62.9 7.4 %all_gather.7 = bf16[1,256,1024]{2,1,0:T(8,128)(2,1)S(1)} all-gather(bf16[1,256,512]{2,1,0:T(8,128)(2,1)} %param.13), channel_id=1, replica_groups=mesh['groups'=2,'ctx'=4,'tensor'=2,'dp'=2] {'tensor'}, dimensions={2}, use_global_device_ids=true | all-gather | bytes 786432 | tf_op jit(solution)/shard_map/all_gather | solution.py:111
  72.4 3.8 scatter_custom_fusion.2
  77.2 21.7 %all-to-all-done = bf16[4,4,192]{2,0,1:T(4,128)(2,1)S(1)} async-done(((bf16[4,4,192]{2,0,1:T(4,128)(2,1)}), bf16[4,4,192]{2,0,1:T(4,128)(2,1)S(1)}, u32[]{:S(2)}, u32[]{:S(2)}) %all-to-all-start) | async-done | bytes 6176 | tf_op jit(solution)/shard_map/all_to_all | solution.py:155
  98.9 4.2 %all-to-all-start.2 = ((bf16[4,4,192,128]{3,2,0,1:T(8,128)(2,1)}), bf16[4,4,192,128]{3,2,0,1:T(8,128)(2,1)}, u32[]{:S(2)}, u32[]{:S(2)}) async-start(bf16[4,4,192,128]{3,2,0,1:T(8,128)(2,1)} %copy.80), calls=%async_computation.3 | async-start | bytes 1572864 | tf_op jit(solution)/shard_map/all_to_all | solution.py:171
  103.4 3.4 maximum_bitcast_fusion
  106.7 3.9 gather_fusion
  110.7 1.9 copy.73
  114.3 23.0 %while.33 = (s32[]{:T(128)}, bf16[3,4,256,128]{3,2,0,1:T(8,128)(2,1)S(1)}, s32[3]{0:T(128)S(1)}, bf16[4,768]{1,0:T(4,128)(2,1)S(1)}, bf16[4,4,192]{2,1,0:T(4,128...) while((s32[]{:T(128)}, ...), condition=%wide.wide.region_8.9_spmd, body=%wide.wide.region_5.8_spmd.sunk | while | flops 612764160 | bytes 3175139 | solution.py:66
  115.7 2.5 fusion.173
  118.2 3.8 fusion.174
  123.3 2.5 fusion.173
  125.9 3.8 fusion.174
  131.0 2.5 fusion.173
  133.5 3.8 fusion.174
  138.3 5.0 %all-to-all-start.1 = ((bf16[4,4,192,128]{3,2,0,1:T(8,128)(2,1)}), bf16[4,4,192,128]{3,2,0,1:T(8,128)(2,1)}, u32[]{:S(2)}, u32[]{:S(2)}) async-start(bf16[4,4,192,128]{3,2,0,1:T(8,128)(2,1)} %copy.76), calls=%async_computation.1 | async-start | bytes 1572864 | tf_op jit(solution)/shard_map/all_to_all | solution.py:163
  143.3 2.1 copy.81
  146.5 56.2 %while.34 = (s32[]{:T(128)}, f32[4,768,128]{2,1,0:T(8,128)S(1)}, f32[4,768,128]{2,1,0:T(8,128)}, bf16[3,4,256,128]{3,2,0,1:T(8,128)(2,1)}, s32[3]{0:T(128)S(1)},...) while((s32[]{:T(128)}, f32[4,768,128]{2,1,0:T(8,128)S(1)}, ...), condition=%wide.wide.region_15.16_spmd.clone, body=%wide.wide.region_11.15_spmd.clone.sunk | while | flops 1222772224 | bytes 25732404 | solution.py:98
  149.0 4.1 %fusion.188 = (f32[4,256]{1,0:T(4,128)S(1)}, f32[4,256,768]{2,1,0:T(8,128)}) fusion(bf16[4,256]{1,0:T(4,128)(2,1)S(1)} %constant_dynamic-slice_fusion.7, bf16[4,768]{1,0:T(4,128)(2,1)S(1)} %get-tuple-element.622, bf16[4,768,128]{2,1,0:T(8,128)(2,1)} %get-tuple-element.618, bf16[4,768,128]{2,1,0:T(8,128)(2,1)} %get-tuple-element.617, ...), kind=kOutput, calls=%fused_computation.133.clone.clone.1 | convolution fusion | flops 205259520 | bytes 4206596 | tf_op jit(solution)/shard_map/vmap()/while/body/eval_jaxpr/sub | solution.py:50
  153.1 3.0 multiply_convert_fusion.3
  157.4 2.2 select_add_fusion.6
  159.7 5.2 %select_add_fusion.7 = f32[4,768,128]{2,1,0:T(8,128)} fusion(f32[4,768,128]{2,1,0:T(8,128)} %get-tuple-element.594, f32[4,256]{1,0:T(4,128)S(1)} %get-tuple-element.531, pred[]{:T(512)S(6)} %compare.29, bf16[4,768,128]{2,1,0:T(8,128)(2,1)} %get-tuple-element.619, s32[]{:T(128)S(1)} %bitcast.245, ...), kind=kOutput, calls=%fused_computation.38.clone.clone.1 | convolution fusion | flops 408160000 | bytes 4469761 | tf_op jit(solution)/shard_map/vmap()/while/body/eval_jaxpr/dot_general | solution.py:40
  167.4 4.1 %fusion.188 = (f32[4,256]{1,0:T(4,128)S(1)}, f32[4,256,768]{2,1,0:T(8,128)}) fusion(bf16[4,256]{1,0:T(4,128)(2,1)S(1)} %constant_dynamic-slice_fusion.7, bf16[4,768]{1,0:T(4,128)(2,1)S(1)} %get-tuple-element.622, bf16[4,768,128]{2,1,0:T(8,128)(2,1)} %get-tuple-element.618, bf16[4,768,128]{2,1,0:T(8,128)(2,1)} %get-tuple-element.617, ...), kind=kOutput, calls=%fused_computation.133.clone.clone.1 | convolution fusion | flops 205259520 | bytes 4206596 | tf_op jit(solution)/shard_map/vmap()/while/body/eval_jaxpr/sub | solution.py:50
  171.5 3.0 multiply_convert_fusion.3
  175.8 2.2 select_add_fusion.6
  178.0 5.7 %select_add_fusion.7 = f32[4,768,128]{2,1,0:T(8,128)} fusion(f32[4,768,128]{2,1,0:T(8,128)} %get-tuple-element.594, f32[4,256]{1,0:T(4,128)S(1)} %get-tuple-element.531, pred[]{:T(512)S(6)} %compare.29, bf16[4,768,128]{2,1,0:T(8,128)(2,1)} %get-tuple-element.619, s32[]{:T(128)S(1)} %bitcast.245, ...), kind=kOutput, calls=%fused_computation.38.clone.clone.1 | convolution fusion | flops 408160000 | bytes 4469761 | tf_op jit(solution)/shard_map/vmap()/while/body/eval_jaxpr/dot_general | solution.py:40
  186.3 4.1 %fusion.188 = (f32[4,256]{1,0:T(4,128)S(1)}, f32[4,256,768]{2,1,0:T(8,128)}) fusion(bf16[4,256]{1,0:T(4,128)(2,1)S(1)} %constant_dynamic-slice_fusion.7, bf16[4,768]{1,0:T(4,128)(2,1)S(1)} %get-tuple-element.622, bf16[4,768,128]{2,1,0:T(8,128)(2,1)} %get-tuple-element.618, bf16[4,768,128]{2,1,0:T(8,128)(2,1)} %get-tuple-element.617, ...), kind=kOutput, calls=%fused_computation.133.clone.clone.1 | convolution fusion | flops 205259520 | bytes 4206596 | tf_op jit(solution)/shard_map/vmap()/while/body/eval_jaxpr/sub | solution.py:50
  190.4 3.0 multiply_convert_fusion.3
  194.7 2.2 select_add_fusion.6
  196.9 5.7 %select_add_fusion.7 = f32[4,768,128]{2,1,0:T(8,128)} fusion(f32[4,768,128]{2,1,0:T(8,128)} %get-tuple-element.594, f32[4,256]{1,0:T(4,128)S(1)} %get-tuple-element.531, pred[]{:T(512)S(6)} %compare.29, bf16[4,768,128]{2,1,0:T(8,128)(2,1)} %get-tuple-element.619, s32[]{:T(128)S(1)} %bitcast.245, ...), kind=kOutput, calls=%fused_computation.38.clone.clone.1 | convolution fusion | flops 408160000 | bytes 4469761 | tf_op jit(solution)/shard_map/vmap()/while/body/eval_jaxpr/dot_general | solution.py:40
  207.4 5.1 %all-to-all-start.3 = ((bf16[4,4,192,384]{3,2,0,1:T(8,128)(2,1)}), bf16[4,4,192,384]{3,2,0,1:T(8,128)(2,1)}, u32[]{:S(2)}, u32[]{:S(2)}) async-start(bf16[4,4,192,384]{3,2,0,1:T(8,128)(2,1)} %copy.84), calls=%async_computation.4 | async-start | bytes 4718592 | tf_op jit(solution)/shard_map/all_to_all | solution.py:179
  213.7 5.8 %gather_fusion.1 = bf16[1024,128]{1,0:T(8,128)(2,1)S(1)} fusion(bf16[4,768,128]{2,1,0:T(8,128)(2,1)S(1)} %bitcast.223, s32[1024]{0:T(1024)S(1)} %bitcast.217), kind=kCustom, calls=%fused_computation.1 | custom fusion | bytes 532480 | tf_op jit(solution)/shard_map/vmap(jit(_take))/gather | solution.py:146
  221.2 43.6 %all-to-all-done.3 = bf16[4,4,192,384]{3,2,0,1:T(8,128)(2,1)} async-done(((bf16[4,4,192,384]{3,2,0,1:T(8,128)(2,1)}), bf16[4,4,192,384]{3,2,0,1:T(8,128)(2,1)}, u32[]{:S(2)}, u32[]{:S(2)}) %all-to-all-start.3) | async-done | bytes 2359328 | tf_op jit(solution)/shard_map/all_to_all | solution.py:179
  264.8 1.9 copy.85
  266.7 11.6 %gather_fusion.2 = bf16[1024,384]{1,0:T(8,128)(2,1)} fusion(bf16[4,768,384]{2,1,0:T(8,128)(2,1)S(1)} %bitcast.219, s32[1024]{0:T(1024)S(1)} %bitcast.218), kind=kCustom, calls=%fused_computation.2 | custom fusion | bytes 1581056 | tf_op jit(solution)/shard_map/vmap(jit(_take))/gather | solution.py:146
  280.8 2.7 convolution_convert_fusion.1
  283.5 4.7 %copy.88 = bf16[1024,3,512]{2,0,1:T(8,128)(2,1)} copy(bf16[1024,3,512]{0,2,1:T(8,128)(2,1)} %bitcast.220) | data formatting | bytes 6291456 | tf_op jit(solution)/shard_map/convert_element_type | solution.py:191
  290.4 3.7 convolution_convert_fusion.5
  294.2 90.2 %all-reduce.3.cloned.1.call-done = (bf16[1024,3,512]{2,0,1:T(8,128)(2,1)}, bf16[512,1024]{1,0:T(8,128)(2,1)}) async-done(((bf16[1024,3,512]{2,0,1:T(8,128)(2,1)}, bf16[512,1024]{1,0:T(8,128)(2,1)}), (bf16[1024,3,512]{2,0,1:T(8,128)(2,1)}, bf16[512,1024]{1,0:T(8,128)(2,1)})) %all-reduce.3.cloned.1.call-update) | async-done | bytes 4194320 | tf_op jit(solution)/shard_map/psum | solution.py:191
  384.4 2.9 convert_element_type.81
  387.3 3.6 convert_element_type.79
  (126 shorter events, 39.9 us)
Async XLA Ops:
  8.0 63.1 %copy-start = (bf16[512,1024]{1,0:T(8,128)(2,1)S(1)}, bf16[512,1024]{1,0:T(8,128)(2,1)}, u32[]{:S(2)}) copy-start(bf16[512,1024]{1,0:T(8,128)(2,1)} %param.11) | copy-start | bytes 3145732
  27.3 4.8 %copy-start.6 = (bf16[1,256,1024]{2,1,0:T(8,128)(2,1)}, bf16[1,256,1024]{2,1,0:T(8,128)(2,1)S(1)}, u32[]{:S(2)}) copy-start(bf16[1,256,1024]{2,1,0:T(8,128)(2,1)S(1)} %all_gather.6) | copy-start | bytes 1572868
  43.6 5.9 %copy-start.11 = (s32[1,4,256]{2,1,0:T(4,128)S(1)}, s32[1,4,256]{2,1,0:T(4,128)}, u32[]{:S(2)}) copy-start(s32[1,4,256]{2,1,0:T(4,128)} %param.12) | copy-start | bytes 12292
  45.1 58.3 %collective-permute-start.2 = (bf16[4,1,192,384]{3,2,0,1:T(8,128)(2,1)}, bf16[4,1,192,384]{3,2,0,1:T(8,128)(2,1)}, u32[]{:S(2)}, u32[]{:S(2)}) collective-permute-start(bf16[4,1,192,384]{3,2,0,1:T(8,128)(2,1)} %get-tuple-element.309), channel_id=1, source_target_pairs={{0,12},{4,8},{8,4},{12,0},{1,13},{5,9},{9,5},{13,1},{2,14},{6,10},... | collective-permute-start | bytes 1769480 | tf_op jit(solution)/shard_map/ppermute | solution.py:28
  48.9 54.5 %collective-permute-start.1 = (bf16[4,1,192,384]{3,2,0,1:T(8,128)(2,1)}, bf16[4,1,192,384]{3,2,0,1:T(8,128)(2,1)}, u32[]{:S(2)}, u32[]{:S(2)}) collective-permute-start(bf16[4,1,192,384]{3,2,0,1:T(8,128)(2,1)} %get-tuple-element.310), channel_id=1, source_target_pairs={{0,8},{4,12},{8,0},{12,4},{1,9},{5,13},{9,1},{13,5},{2,10},{6,14},... | collective-permute-start | bytes 1769480 | tf_op jit(solution)/shard_map/ppermute | solution.py:28
  48.9 54.5 %collective-permute-start = (bf16[4,1,192,384]{3,2,0,1:T(8,128)(2,1)}, bf16[4,1,192,384]{3,2,0,1:T(8,128)(2,1)}, u32[]{:S(2)}, u32[]{:S(2)}) collective-permute-start(bf16[4,1,192,384]{3,2,0,1:T(8,128)(2,1)} %get-tuple-element.311), channel_id=1, source_target_pairs={{0,4},{4,0},{8,12},{12,8},{1,5},{5,1},{9,13},{13,9},{2,6},{6,2},{1... | collective-permute-start | bytes 1769480 | tf_op jit(solution)/shard_map/ppermute | solution.py:28
  57.8 41.1 %all-to-all-start = ((bf16[4,4,192]{2,0,1:T(4,128)(2,1)}), bf16[4,4,192]{2,0,1:T(4,128)(2,1)S(1)}, u32[]{:S(2)}, u32[]{:S(2)}) async-start(bf16[4,4,192]{2,0,1:T(4,128)(2,1)} %copy.68), calls=%async_computation | async-start | bytes 16384 | tf_op jit(solution)/shard_map/all_to_all | solution.py:155
  70.3 0.8 copy-start.1
  98.9 39.4 %all-to-all-start.2 = ((bf16[4,4,192,128]{3,2,0,1:T(8,128)(2,1)}), bf16[4,4,192,128]{3,2,0,1:T(8,128)(2,1)}, u32[]{:S(2)}, u32[]{:S(2)}) async-start(bf16[4,4,192,128]{3,2,0,1:T(8,128)(2,1)} %copy.80), calls=%async_computation.3 | async-start | bytes 1572864 | tf_op jit(solution)/shard_map/all_to_all | solution.py:171
  103.1 3.7 copy-start.10
  138.3 69.1 %all-to-all-start.1 = ((bf16[4,4,192,128]{3,2,0,1:T(8,128)(2,1)}), bf16[4,4,192,128]{3,2,0,1:T(8,128)(2,1)}, u32[]{:S(2)}, u32[]{:S(2)}) async-start(bf16[4,4,192,128]{3,2,0,1:T(8,128)(2,1)} %copy.76), calls=%async_computation.1 | async-start | bytes 1572864 | tf_op jit(solution)/shard_map/all_to_all | solution.py:163
  153.1 3.0 copy-start.9
  171.5 3.0 copy-start.9
  190.4 3.0 copy-start.9
  202.7 1.4 copy-start.8
  207.4 57.5 %all-to-all-start.3 = ((bf16[4,4,192,384]{3,2,0,1:T(8,128)(2,1)}), bf16[4,4,192,384]{3,2,0,1:T(8,128)(2,1)}, u32[]{:S(2)}, u32[]{:S(2)}) async-start(bf16[4,4,192,384]{3,2,0,1:T(8,128)(2,1)} %copy.84), calls=%async_computation.4 | async-start | bytes 4718592 | tf_op jit(solution)/shard_map/all_to_all | solution.py:179
  212.5 171.9 %all-reduce.3.cloned.1.call-start = ((), (), s32[]{:S(2)}) async-start(), calls=%async_computation.8 | async-start | bytes 8388608 | tf_op jit(solution)/shard_map/psum | solution.py:191
  213.7 6.1 %copy-start.2 = (bf16[1,256,1024]{2,1,0:T(8,128)(2,1)S(1)}, bf16[1,256,1024]{2,1,0:T(8,128)(2,1)}, u32[]{:S(2)}) copy-start(bf16[1,256,1024]{2,1,0:T(8,128)(2,1)} %copy-done.1) | copy-start | bytes 1572868
  219.7 1.4 copy-start.4
  279.7 1.1 copy-start.7
  288.1 0.9 copy-start.5
  288.2 102.7 %reduce-scatter.3.cloned.1.call-start = ((), (), s32[]{:S(2)}) async-start(), calls=%async_computation.6 | async-start | bytes 786432 | tf_op jit(solution)/shard_map/reduce_scatter | solution.py:183
  290.4 100.5 %reduce-scatter.5.cloned.1.call-start = ((), (), s32[]{:S(2)}) async-start(), calls=%async_computation.7 | async-start | bytes 786432 | tf_op jit(solution)/shard_map/reduce_scatter | solution.py:195
  384.4 2.9 copy-start.3
Sparse Core Ops, SparseCore 0:
  288.3 96.0 all-reduce.2
Sparse Core Ops, SparseCore 1:
  291.5 13.6 reduce-scatter.2
  307.9 14.5 reduce-scatter.4
